TPU v7x, 512 devices: a whole 4x8x8 slice. The times are simulated.
512 devices in a mesh: head: 4 (over x), tensor: 16 (over y, z_hi), dp: 8 (over z_lo, core).
Axes of the slice: x: 4, y: 8, z: 8 (z_hi: 2, z_lo: 4; z = z_hi * 4 + z_lo), core: 2. Of those that a mesh axis runs over, the one named last changes fastest.
Arguments:
- trunk_hidden: bfloat16 [384, 5120], P('dp', 'tensor'), may hold values from -60 to 60
- next_embeds: bfloat16 [4, 384, 5120], P('head', 'dp', 'tensor'), may hold values from -6 to 6
- combine_weight: bfloat16 [4, 10240, 5120], P('head', 'dp', 'tensor'), may hold values from -0.0625 to 0.0625
- final_gain: float32 [5120], P('tensor'), may hold values from 0.5 to 1.5
- unembed_weight: bfloat16 [16384, 5120], P('dp', 'tensor'), may hold values from -32 to 32
- target_ids: int32 [4, 384], P('head'), may hold values from 0 to 16383
- loss_scale: float32 [4, 384], P('head'), may hold values from 2 to 32
Outputs:
- trunk_grad: float32 [384, 5120], P('dp', 'tensor')
- embed_grad: float32 [4, 384, 5120], P('head', 'dp', 'tensor')
- combine_grad: float32 [4, 10240, 5120], P('head', 'dp', 'tensor')
- unembed_grad: float32 [8, 4, 512, 5120], P('dp', 'head', None, 'tensor')
All inputs are finite; a program needn't handle non-finite values.
Results may differ from a plain program's by a relative error of at most 0.02.
Values may be sent and summed in bfloat16 or wider, within the bound.
A program may use at most 64 MiB of HBM per device.

v0:
```python
import jax
import jax.numpy as jnp
from jax import lax
from jax.sharding import PartitionSpec as P

D = 5120
epsilon = 1e-05


def contract_rows(left, right):
    return lax.dot_general(
        left, right, (((0,), (0,)), ((), ())), preferred_element_type=jnp.float32
    )


def contract_cols(left, right):
    return lax.dot_general(
        left, right, (((1,), (1,)), ((), ())), preferred_element_type=jnp.float32
    )


def local(
    trunk_hidden, next_embeds, combine_weight, final_gain, unembed_weight, target_ids, loss_scale
):
    rows, part_width = trunk_hidden.shape
    vocab_part = unembed_weight.shape[0]
    weight_block = combine_weight[0]
    trunk_whole, embed_whole = (
        lax.all_gather(trunk_hidden, "tensor", axis=1, tiled=True),
        lax.all_gather(next_embeds[0], "tensor", axis=1, tiled=True),
    )
    trunk_float = trunk_whole.astype(jnp.float32)
    embed_float = embed_whole.astype(jnp.float32)
    trunk_scale = lax.rsqrt(jnp.sum(trunk_float * trunk_float, axis=1) / D + epsilon)
    embed_scale = lax.rsqrt(jnp.sum(embed_float * embed_float, axis=1) / D + epsilon)
    trunk_normed = trunk_float * trunk_scale[:, None]
    embed_normed = embed_float * embed_scale[:, None]
    joined = jnp.concatenate(
        [trunk_normed.astype(jnp.bfloat16), embed_normed.astype(jnp.bfloat16)], axis=1
    )
    feature_start = lax.axis_index("tensor") * part_width
    trunk_local = lax.dynamic_slice_in_dim(trunk_normed, feature_start, part_width, 1)
    embed_local = lax.dynamic_slice_in_dim(embed_normed, feature_start, part_width, 1)
    blocks = lax.all_to_all(joined, "dp", split_axis=1, concat_axis=0, tiled=True)
    weight_whole = lax.all_gather(weight_block, "dp", axis=0, tiled=True)
    projected = jnp.dot(joined, weight_whole, preferred_element_type=jnp.float32)
    mixed = trunk_hidden.astype(jnp.float32) + projected
    mixed_sums = lax.psum(jnp.sum(mixed * mixed, axis=1), "tensor")
    mixed_scale = lax.rsqrt(mixed_sums / D + epsilon)
    mixed_normed = mixed * mixed_scale[:, None]
    normed_out = (mixed_normed * final_gain[None, :]).astype(jnp.bfloat16)
    normed_all = lax.all_gather(normed_out, "dp", axis=0, tiled=True)
    partial_logits = contract_cols(normed_all, unembed_weight)
    logits = lax.psum(partial_logits, "tensor")
    row_targets = target_ids[0]
    row_weights = loss_scale[0]
    largest = lax.pmax(jnp.max(logits, axis=1), "dp")
    shifted = jnp.exp(logits - largest[:, None])
    summed = lax.psum(jnp.sum(shifted, axis=1), "dp")
    probs = shifted / summed[:, None]
    vocab_ids = (
        lax.broadcasted_iota(jnp.int32, (1, vocab_part), 1) + lax.axis_index("dp") * vocab_part
    )
    hits = (vocab_ids == row_targets[:, None]).astype(jnp.float32)
    grad_local = (row_weights[:, None] * (probs - hits)).astype(jnp.bfloat16)
    grad_normed = lax.psum_scatter(
        jnp.dot(grad_local, unembed_weight, preferred_element_type=jnp.float32).astype(
            jnp.bfloat16
        ),
        "dp",
        scatter_dimension=0,
        tiled=True,
    ).astype(jnp.float32)
    vocab_term = contract_rows(grad_local, normed_all).astype(jnp.bfloat16)
    vocab_total = lax.psum_scatter(vocab_term, "head", scatter_dimension=0, tiled=True).astype(
        jnp.float32
    )
    unembed_grad = vocab_total.reshape(1, 1, vocab_total.shape[0], part_width)
    scaled_grad = grad_normed * final_gain[None, :]
    grad_dots = lax.psum(jnp.sum(scaled_grad * mixed_normed, axis=1), "tensor")
    grad_mixed = mixed_scale[:, None] * (scaled_grad - mixed_normed * (grad_dots / D)[:, None])
    grad_mixed_low = grad_mixed.astype(jnp.bfloat16)
    grad_all = lax.all_gather(grad_mixed_low, "dp", axis=0, tiled=True)
    combine_grad = contract_rows(blocks, grad_all)[None]
    joined_part = contract_cols(grad_mixed_low, weight_whole)
    joined_grad = lax.psum_scatter(
        joined_part.reshape(rows, 2, D).astype(jnp.bfloat16),
        "tensor",
        scatter_dimension=2,
        tiled=True,
    ).astype(jnp.float32)
    trunk_side = joined_grad[:, 0]
    embed_side = joined_grad[:, 1]
    trunk_dots, embed_dots = lax.psum(
        (jnp.sum(trunk_side * trunk_local, axis=1), jnp.sum(embed_side * embed_local, axis=1)),
        "tensor",
    )
    trunk_term = trunk_scale[:, None] * (trunk_side - trunk_local * (trunk_dots / D)[:, None])
    embed_grad = (embed_scale[:, None] * (embed_side - embed_local * (embed_dots / D)[:, None]))[
        None
    ]
    trunk_grad = lax.psum((grad_mixed + trunk_term).astype(jnp.bfloat16), "head").astype(
        jnp.float32
    )
    return (trunk_grad, embed_grad, combine_grad, unembed_grad)


def solution(mesh):
    in_specs = (
        P("dp", "tensor"),
        P("head", "dp", "tensor"),
        P("head", "dp", "tensor"),
        P("tensor"),
        P("dp", "tensor"),
        P("head", None),
        P("head", None),
    )
    out_specs = (
        P("dp", "tensor"),
        P("head", "dp", "tensor"),
        P("head", "dp", "tensor"),
        P("dp", "head", None, "tensor"),
    )
    return jax.shard_map(local, mesh=mesh, in_specs=in_specs, out_specs=out_specs, check_vma=False)
```

profile of v0, /device:TPU:32, one launch (start us, length us, event | category | flops | bytes accessed | tf_op | source)
XLA Modules:
  0.0 1121.4 jit_solution(15558136090920150623)
XLA Ops:
  7.2 0.7 all-gather.5.cloned.1.call-update
  8.0 69.0 %all-gather.2 = bf16[16,320,48]{1,2,0:T(8,128)(2,1)S(1)} all-gather(bf16[1,320,48]{1,2,0:T(8,128)(2,1)} %bitcast.77), channel_id=1, replica_groups=mesh['head'=4,'tensor'=16,'dp'=8] {'tensor'}, dimensions={0}, use_global_device_ids=true | all-gather | bytes 522240 | tf_op jit(solution)/shard_map/all_gather | solution.py:29
  76.9 0.1 copy.15
  77.1 0.3 reshape.52
  77.4 0.2 copy.16
  77.6 160.0 %all-gather = bf16[1,48,5120]{1,0,2:T(2,128)(2,1)} all-gather(bf16[1,48,320]{1,0,2:T(2,128)(2,1)S(1)} %copy.16), channel_id=2, replica_groups=mesh['head'=4,'tensor'=16,'dp'=8] {'tensor'}, dimensions={2}, use_global_device_ids=true | all-gather | bytes 522240 | tf_op jit(solution)/shard_map/all_gather | solution.py:30
  237.6 4.7 copy.17
  242.4 0.2 fusion.7
  242.6 0.2 multiply_reduce_fusion
  242.8 1.2 convert_multiply_fusion
  244.0 1.2 convert_bitcast_fusion
  245.2 5.1 multiply_reduce_fusion.3
  250.3 52.9 %psum.49 = f32[48]{0:T(128)S(1)} all-reduce(f32[48]{0:T(128)S(1)} %get-tuple-element.14), channel_id=1, replica_groups=mesh['head'=4,'tensor'=16,'dp'=8] {'tensor'}, use_global_device_ids=true, to_apply=%region_3.0 | all-reduce | flops 48 | bytes 384 | tf_op jit(solution)/shard_map/psum | solution.py:48
  303.3 0.1 multiply_convert_fusion.1
  303.3 17.8 %all_gather.18 = bf16[384,320]{1,0:T(8,128)(2,1)S(1)} all-gather(bf16[48,320]{1,0:T(8,128)(2,1)S(1)} %multiply_convert_fusion.1), channel_id=1, replica_groups=mesh['head'=4,'tensor'=16,'dp'=8] {'dp'}, dimensions={0}, use_global_device_ids=true | all-gather | bytes 276480 | tf_op jit(solution)/shard_map/all_gather | solution.py:52
  321.2 0.7 copy-done.2
  321.9 2.6 fusion.15
  324.6 0.6 copy-done.7
  325.3 340.8 %all-reduce.3.cloned.1.call-done = f32[384,2048]{1,0:T(8,128)} async-done(((f32[384,2048]{1,0:T(8,128)}), f32[384,2048]{1,0:T(8,128)}) %all-reduce.3.cloned.1.call-update) | async-done | bytes 3145744 | tf_op jit(solution)/shard_map/psum | solution.py:54
  666.1 2.1 reduce_max.9
  668.2 13.6 %pmax.7 = f32[384]{0:T(512)S(1)} all-reduce(f32[384]{0:T(512)S(1)} %reduce_max.9), channel_id=1, replica_groups=mesh['head'=4,'tensor'=16,'dp'=8] {'dp'}, use_global_device_ids=true, to_apply=%region_6.0 | all-reduce | flops 384 | bytes 3072 | tf_op jit(solution)/shard_map/pmax | solution.py:57
  681.8 2.5 fusion.3
  684.3 13.6 %psum.51 = f32[384]{0:T(512)S(1)} all-reduce(f32[384]{0:T(512)S(1)} %fusion.3), channel_id=1, replica_groups=mesh['head'=4,'tensor'=16,'dp'=8] {'dp'}, use_global_device_ids=true, to_apply=%region_8.0 | all-reduce | flops 384 | bytes 3072 | tf_op jit(solution)/shard_map/psum | solution.py:59
  697.9 2.9 multiply_convert_fusion
  700.7 1.7 convolution_convert_fusion.2
  702.5 40.0 %reduce-scatter.6.cloned.1.call-done = bf16[48,320]{1,0:T(8,128)(2,1)} async-done(((bf16[384,320]{1,0:T(8,128)(2,1)}), bf16[48,320]{1,0:T(8,128)(2,1)}) %reduce-scatter.6.cloned.1.call-update) | async-done | bytes 30736 | tf_op jit(solution)/shard_map/reduce_scatter | solution.py:66
  742.5 0.9 multiply_reduce_fusion.2
  743.4 49.8 %psum.52 = f32[48]{0:T(128)S(1)} all-reduce(f32[48]{0:T(128)S(1)} %multiply_reduce_fusion.2), channel_id=1, replica_groups=mesh['head'=4,'tensor'=16,'dp'=8] {'tensor'}, use_global_device_ids=true, to_apply=%region_11.0 | all-reduce | flops 48 | bytes 384 | tf_op jit(solution)/shard_map/psum | solution.py:80
  793.3 0.9 fusion.13
  794.1 5.1 convolution_convert_fusion
  799.2 3.7 convert_element_type.64
  802.9 7.5 copy.20
  810.4 5.4 reshape.53
  815.8 2.9 convolution_convert_fusion.1
  818.8 1.1 pad_maximum_fusion
  819.9 1.0 copy.25
  820.9 3.6 all-to-all-start
  824.5 34.0 %all_gather.19 = bf16[384,320]{1,0:T(8,128)(2,1)S(1)} all-gather(bf16[48,320]{1,0:T(8,128)(2,1)S(1)} %fusion.13), channel_id=1, replica_groups=mesh['head'=4,'tensor'=16,'dp'=8] {'dp'}, dimensions={0}, use_global_device_ids=true | all-gather | bytes 276480 | tf_op jit(solution)/shard_map/all_gather | solution.py:83
  858.5 1.8 convolution_bitcast_fusion
  860.3 182.5 %reduce-scatter.10.cloned.1.call-done = bf16[320,96]{1,0:T(8,128)(2,1)} async-done(((bf16[5120,96]{1,0:T(8,128)(2,1)}), bf16[320,96]{1,0:T(8,128)(2,1)}) %reduce-scatter.10.cloned.1.call-update) | async-done | bytes 61456
  1042.8 1.0 reshape.54
  1043.8 0.1 copy.21
  1043.9 1.2 multiply_reduce_fusion.1
  1045.1 48.3 %all-reduce = (f32[48]{0:T(128)S(1)}, f32[48]{0:T(128)S(1)}) all-reduce(f32[48]{0:T(128)S(1)} %get-tuple-element.5, f32[48]{0:T(128)S(1)} %get-tuple-element.4), channel_id=1, replica_groups=mesh['head'=4,'tensor'=16,'dp'=8] {'tensor'}, use_global_device_ids=true, to_apply=%region_14.0 | all-reduce | flops 96 | bytes 768 | tf_op jit(solution)/shard_map/psum | solution.py:94
  1093.3 1.7 multiply_bitcast_fusion
  1095.1 17.3 %psum.54 = bf16[48,320]{1,0:T(8,128)(2,1)S(1)} all-reduce(bf16[48,320]{1,0:T(8,128)(2,1)S(1)} %get-tuple-element.13), channel_id=1, replica_groups=mesh['head'=4,'tensor'=16,'dp'=8] {'head'}, use_global_device_ids=true, to_apply=%region_15.0 | all-reduce | flops 15360 | bytes 61440 | tf_op jit(solution)/shard_map/psum | solution.py:102
  1112.4 0.6 convert_element_type.67
  1113.0 1.9 bitcast_convert_fusion
  (37 shorter events, 0.4 us)
Async XLA Ops:
  7.2 314.8 %copy-start = (bf16[2048,320]{0,1:T(8,128)(2,1)S(1)}, bf16[2048,320]{0,1:T(8,128)(2,1)}, u32[]{:S(2)}) copy-start(bf16[2048,320]{0,1:T(8,128)(2,1)} %param.11) | copy-start | bytes 3932164
  7.2 70.2 %copy-start.5 = (bf16[1,48,320]{2,1,0:T(8,128)(2,1)S(1)}, bf16[1,48,320]{2,1,0:T(8,128)(2,1)}, u32[]{:S(2)}) copy-start(bf16[1,48,320]{2,1,0:T(8,128)(2,1)} %param.8) | copy-start | bytes 92164
  7.2 238.0 %all-gather.5.cloned.1.call-start = ((), (), s32[]{:S(2)}) async-start(), calls=%async_computation.7 | async-start | bytes 7372800 | tf_op jit(solution)/shard_map/all_gather | solution.py:45
  7.9 658.2 %all-reduce.3.cloned.1.call-start = ((), (), s32[]{:S(2)}) async-start(), calls=%async_computation.4 | async-start | bytes 6291456 | tf_op jit(solution)/shard_map/psum | solution.py:54
  242.6 2.6 copy-start.4
  245.1 5.2 copy-start.1
  245.2 58.1 %copy-start.6 = (f32[320]{0:T(512)S(1)}, f32[320]{0:T(512)}, u32[]{:S(2)}) copy-start(f32[320]{0:T(512)} %param.10) | copy-start | bytes 3844
  321.2 0.7 copy-start.2
  324.5 0.7 copy-start.7
  324.5 0.7 copy-start.8
  324.6 417.9 %reduce-scatter.6.cloned.1.call-start = ((), (), s32[]{:S(2)}) async-start(), calls=%async_computation.5 | async-start | bytes 331776 | tf_op jit(solution)/shard_map/reduce_scatter | solution.py:66
  702.5 340.3 %reduce-scatter.10.cloned.1.call-start = ((), (), s32[]{:S(2)}) async-start(), calls=%async_computation.8 | async-start | bytes 1392640
  815.8 297.2 %reduce-scatter.8.cloned.1.call-start = ((), (), s32[]{:S(2)}) async-start(), calls=%async_computation.6 | async-start | bytes 1638400 | tf_op jit(solution)/shard_map/reduce_scatter | solution.py:75
  820.9 37.6 %all-to-all-start = ((bf16[48,8,1280]{2,0,1:T(8,128)(2,1)}), bf16[48,8,1280]{2,0,1:T(8,128)(2,1)S(1)}, u32[]{:S(2)}, u32[]{:S(2)}) async-start(bf16[48,8,1280]{2,0,1:T(8,128)(2,1)} %bitcast.72), calls=%async_computation.1 | async-start | bytes 1966080 | tf_op jit(solution)/shard_map/all_to_all | solution.py:44
  824.4 268.9 %copy-start.3 = (bf16[48,320]{1,0:T(8,128)(2,1)S(1)}, bf16[48,320]{1,0:T(8,128)(2,1)}, u32[]{:S(2)}) copy-start(bf16[48,320]{1,0:T(8,128)(2,1)} %reduce-scatter.6.cloned.1.call-done) | copy-start | bytes 92164
Sparse Core Ops, SparseCore 0:
  10.1 162.1 all-gather.4
  324.7 341.3 all-reduce.2
  702.6 39.8 reduce-scatter.5
  815.9 226.8 reduce-scatter.9
  1045.5 26.0 reduce-scatter.7
where the time goes:
time: 1120 us
  waiting for transfers between devices  564 us (50%)
  blocking collectives  476 us (42%)
  local copies, waits for them, and re-layouts  25.4 us (2%)
  matrix products  19.3 us (2%)
  other arithmetic  18.7 us (2%)
  between operations  14 us (1%)
    psum x1, waiting for transfers between devices, local(): logits = lax.psum(partial_logits, 'tensor')  341 us
    unnamed x6, waiting for transfers between devices  183 us
    all_gather x1, blocking collectives, local(): lax.all_gather(next_embeds[0], 'tensor', axis=1, tiled=True)  160 us
    all_gather x1, blocking collectives, local(): lax.all_gather(trunk_hidden, 'tensor', axis=1, tiled=True)  69 us
    psum x1, blocking collectives, local(): mixed_sums = lax.psum(jnp.sum(mixed * mixed, axis=1), 'tensor')  52.9 us
    psum x1, blocking collectives, local(): grad_dots = lax.psum(jnp.sum(scaled_grad * mixed_normed, axis=1), 'tensor')  49.8 us
    psum x1, blocking collectives, local(): lax.psum((jnp.sum(trunk_side * trunk_local, axis=1), jnp.sum(embed_side *...  48.3 us
    reduce_scatter x1, waiting for transfers between devices, local(): lax.psum_scatter(jnp.dot(grad_local, unembed_weight, preferred_element_ty...  40 us
  transfers between devices with their start and end apart: 6, of which 3 were waited for; matrix products, arithmetic and copies ran while one was open for 2% of the time, Pallas kernels for 0%

commit v1 on v0

--- a/solution.py
+++ b/solution.py
@@ -5,6 +5,11 @@
 
 D = 5120
 epsilon = 1e-05
+
+
+def all_by_exchange(x, axis, dim):
+    stack = jnp.stack([x] * lax.axis_size(axis))
+    return jnp.concatenate(lax.all_to_all(stack, axis, 0, 0), axis=dim)
 
 
 def contract_rows(left, right):
@@ -27,7 +32,7 @@
     weight_block = combine_weight[0]
     trunk_whole, embed_whole = (
         lax.all_gather(trunk_hidden, "tensor", axis=1, tiled=True),
-        lax.all_gather(next_embeds[0], "tensor", axis=1, tiled=True),
+        all_by_exchange(next_embeds[0], "tensor", 1),
     )
     trunk_float = trunk_whole.astype(jnp.float32)
     embed_float = embed_whole.astype(jnp.float32)

time: 1120 us -> 995 us (0.89)
  blocking collectives: 476 us -> 318 us
  starting transfers between devices: 3.76 us -> 19.4 us
  waiting for transfers between devices: 564 us -> 577 us
    all_gather x1 -> x0, blocking collectives: 160 us -> none  [local(): lax.all_gather(next_embeds[0], 'tensor', axis=1, tiled=True)]
    all_gather x1, waiting for transfers between devices: 0.01 us -> 18.7 us  [local(): weight_whole = lax.all_gather(weight_block, 'dp', axis=0, tiled=True)]
    all_to_all x0 -> x1, starting transfers between devices: none -> 15.7 us  [all_by_exchange(): return jnp.concatenate(lax.all_to_all(stack, axis, 0, 0), axis=dim)]
  transfers between devices with their start and end apart: 6 -> 7, of which waited for: 3 -> 4; matrix products, arithmetic and copies ran while one was open for 2% -> 2% of each run, Pallas kernels for 0% -> 0%
where the time goes in v1:
time: 995 us; the launch traced here: 994 us
  waiting for transfers between devices  577 us (58%)
  blocking collectives  318 us (32%)
  local copies, waits for them, and re-layouts  26.1 us (3%)
  other arithmetic  20.2 us (2%)
  starting transfers between devices  19.4 us (2%)
  matrix products  19.1 us (2%)
  between operations  13.9 us (1%)
    psum x1, waiting for transfers between devices, local(): logits = lax.psum(partial_logits, 'tensor')  334 us
    unnamed x6, waiting for transfers between devices  183 us
    all_gather x1, blocking collectives, local(): lax.all_gather(trunk_hidden, 'tensor', axis=1, tiled=True)  76.7 us
    psum x1, blocking collectives, local(): mixed_sums = lax.psum(jnp.sum(mixed * mixed, axis=1), 'tensor')  49.9 us
    psum x1, blocking collectives, local(): grad_dots = lax.psum(jnp.sum(scaled_grad * mixed_normed, axis=1), 'tensor')  49.9 us
    psum x1, blocking collectives, local(): lax.psum((jnp.sum(trunk_side * trunk_local, axis=1), jnp.sum(embed_side *...  48.3 us
    reduce_scatter x1, waiting for transfers between devices, local(): lax.psum_scatter(jnp.dot(grad_local, unembed_weight, preferred_element_ty...  41.4 us
    all_gather x1, blocking collectives, local(): grad_all = lax.all_gather(grad_mixed_low, 'dp', axis=0, tiled=True)  34.1 us
  transfers between devices with their start and end apart: 7, of which 4 were waited for; matrix products, arithmetic and copies ran while one was open for 2% of the time, Pallas kernels for 0%

profile of v1, /device:TPU:32, one launch (start us, length us, event | category | flops | bytes accessed | tf_op | source)
XLA Modules:
  0.0 993.7 jit_solution(7290781713229587160)
XLA Ops:
  7.2 0.7 all-gather.4.cloned.1.call-update
  7.9 1.6 stack.3
  9.6 15.7 %all-to-all-start = ((bf16[16,48,320]{2,1,0:T(8,128)(2,1)}), bf16[16,48,320]{2,1,0:T(8,128)(2,1)S(1)}, u32[]{:S(2)}, u32[]{:S(2)}) async-start(bf16[16,48,320]{2,1,0:T(8,128)(2,1)} %stack.3), calls=%async_computation | async-start | bytes 1179648 | tf_op jit(solution)/shard_map/all_to_all | solution.py:12
  25.3 76.7 %all-gather.1 = bf16[16,320,48]{1,2,0:T(8,128)(2,1)S(1)} all-gather(bf16[1,320,48]{1,2,0:T(8,128)(2,1)S(1)} %bitcast.74), channel_id=1, replica_groups=mesh['head'=4,'tensor'=16,'dp'=8] {'tensor'}, dimensions={0}, use_global_device_ids=true | all-gather | bytes 522240 | tf_op jit(solution)/shard_map/all_gather | solution.py:34
  102.0 1.1 copy.15
  103.2 1.6 reshape.56
  104.8 0.2 multiply_reduce_fusion
  105.0 1.3 convert_bitcast_fusion.1
  106.4 0.4 copy.16
  106.8 1.3 reshape.50
  108.1 0.2 fusion.4
  108.3 2.4 fusion.14
  110.7 18.7 %all-gather.4.cloned.1.call-done = bf16[1,10240,320]{1,2,0:T(8,128)(2,1)} async-done(((bf16[1,1280,320]{1,2,0:T(8,128)(2,1)}), bf16[1,10240,320]{1,2,0:T(8,128)(2,1)}) %all-gather.4.cloned.1.call-update) | async-done | bytes 6553616 | tf_op jit(solution)/shard_map/all_gather | solution.py:50
  129.4 5.0 multiply_reduce_fusion.3
  134.4 49.9 %psum.49 = f32[48]{0:T(128)S(1)} all-reduce(f32[48]{0:T(128)S(1)} %get-tuple-element.14), channel_id=1, replica_groups=mesh['head'=4,'tensor'=16,'dp'=8] {'tensor'}, use_global_device_ids=true, to_apply=%region_3.0 | all-reduce | flops 48 | bytes 384 | tf_op jit(solution)/shard_map/psum | solution.py:53
  184.4 14.3 %all_gather.14 = bf16[384,320]{1,0:T(8,128)(2,1)S(1)} all-gather(bf16[48,320]{1,0:T(8,128)(2,1)S(1)} %multiply_convert_fusion.1), channel_id=1, replica_groups=mesh['head'=4,'tensor'=16,'dp'=8] {'dp'}, dimensions={0}, use_global_device_ids=true | all-gather | bytes 276480 | tf_op jit(solution)/shard_map/all_gather | solution.py:57
  198.6 0.7 copy-done.3
  199.4 2.6 fusion.15
  202.1 0.6 copy-done.7
  202.7 334.4 %all-reduce.3.cloned.1.call-done = f32[384,2048]{1,0:T(8,128)} async-done(((f32[384,2048]{1,0:T(8,128)}), f32[384,2048]{1,0:T(8,128)}) %all-reduce.3.cloned.1.call-update) | async-done | bytes 3145744 | tf_op jit(solution)/shard_map/psum | solution.py:59
  537.1 2.1 reduce_max.9
  539.2 13.6 %pmax.7 = f32[384]{0:T(512)S(1)} all-reduce(f32[384]{0:T(512)S(1)} %reduce_max.9), channel_id=1, replica_groups=mesh['head'=4,'tensor'=16,'dp'=8] {'dp'}, use_global_device_ids=true, to_apply=%region_6.0 | all-reduce | flops 384 | bytes 3072 | tf_op jit(solution)/shard_map/pmax | solution.py:62
  552.8 2.5 fusion.3
  555.2 13.6 %psum.51 = f32[384]{0:T(512)S(1)} all-reduce(f32[384]{0:T(512)S(1)} %fusion.3), channel_id=1, replica_groups=mesh['head'=4,'tensor'=16,'dp'=8] {'dp'}, use_global_device_ids=true, to_apply=%region_8.0 | all-reduce | flops 384 | bytes 3072 | tf_op jit(solution)/shard_map/psum | solution.py:64
  568.8 2.9 multiply_convert_fusion
  571.7 1.7 convolution_convert_fusion.2
  573.5 41.4 %reduce-scatter.6.cloned.1.call-done = bf16[48,320]{1,0:T(8,128)(2,1)} async-done(((bf16[384,320]{1,0:T(8,128)(2,1)}), bf16[48,320]{1,0:T(8,128)(2,1)}) %reduce-scatter.6.cloned.1.call-update) | async-done | bytes 30736 | tf_op jit(solution)/shard_map/reduce_scatter | solution.py:71
  614.9 0.9 multiply_reduce_fusion.2
  615.9 49.9 %psum.52 = f32[48]{0:T(128)S(1)} all-reduce(f32[48]{0:T(128)S(1)} %multiply_reduce_fusion.2), channel_id=1, replica_groups=mesh['head'=4,'tensor'=16,'dp'=8] {'tensor'}, use_global_device_ids=true, to_apply=%region_11.0 | all-reduce | flops 48 | bytes 384 | tf_op jit(solution)/shard_map/psum | solution.py:85
  665.7 0.9 fusion.13
  666.6 5.1 convolution_convert_fusion
  671.7 3.7 convert_element_type.77
  675.4 7.5 copy.19
  682.8 5.4 reshape.57
  688.3 2.9 convolution_convert_fusion.1
  691.2 1.1 pad_maximum_fusion
  692.3 1.0 copy.24
  693.3 3.6 all-to-all-start.1
  696.9 34.1 %all_gather.15 = bf16[384,320]{1,0:T(8,128)(2,1)S(1)} all-gather(bf16[48,320]{1,0:T(8,128)(2,1)S(1)} %fusion.13), channel_id=1, replica_groups=mesh['head'=4,'tensor'=16,'dp'=8] {'dp'}, dimensions={0}, use_global_device_ids=true | all-gather | bytes 276480 | tf_op jit(solution)/shard_map/all_gather | solution.py:88
  731.0 1.8 convolution_bitcast_fusion
  732.8 182.2 %reduce-scatter.10.cloned.1.call-done = bf16[320,96]{1,0:T(8,128)(2,1)} async-done(((bf16[5120,96]{1,0:T(8,128)(2,1)}), bf16[320,96]{1,0:T(8,128)(2,1)}) %reduce-scatter.10.cloned.1.call-update) | async-done | bytes 61456
  915.0 1.0 reshape.58
  916.1 1.2 multiply_reduce_fusion.1
  917.3 48.3 %all-reduce = (f32[48]{0:T(128)S(1)}, f32[48]{0:T(128)S(1)}) all-reduce(f32[48]{0:T(128)S(1)} %get-tuple-element.5, f32[48]{0:T(128)S(1)} %get-tuple-element.4), channel_id=1, replica_groups=mesh['head'=4,'tensor'=16,'dp'=8] {'tensor'}, use_global_device_ids=true, to_apply=%region_14.0 | all-reduce | flops 96 | bytes 768 | tf_op jit(solution)/shard_map/psum | solution.py:99
  965.6 1.7 multiply_bitcast_fusion
  967.3 17.3 %psum.54 = bf16[48,320]{1,0:T(8,128)(2,1)S(1)} all-reduce(bf16[48,320]{1,0:T(8,128)(2,1)S(1)} %get-tuple-element.13), channel_id=1, replica_groups=mesh['head'=4,'tensor'=16,'dp'=8] {'head'}, use_global_device_ids=true, to_apply=%region_15.0 | all-reduce | flops 15360 | bytes 61440 | tf_op jit(solution)/shard_map/psum | solution.py:107
  984.6 0.6 convert_element_type.80
  985.2 1.9 bitcast_convert_fusion
  (40 shorter events, 0.7 us)
Async XLA Ops:
  7.2 192.2 %copy-start = (bf16[2048,320]{0,1:T(8,128)(2,1)S(1)}, bf16[2048,320]{0,1:T(8,128)(2,1)}, u32[]{:S(2)}) copy-start(bf16[2048,320]{0,1:T(8,128)(2,1)} %param.11) | copy-start | bytes 3932164
  7.2 18.1 %copy-start.5 = (bf16[48,320]{1,0:T(8,128)(2,1)S(1)}, bf16[48,320]{1,0:T(8,128)(2,1)}, u32[]{:S(2)}) copy-start(bf16[48,320]{1,0:T(8,128)(2,1)} %param.7) | copy-start | bytes 92164
  7.2 122.2 %all-gather.4.cloned.1.call-start = ((), (), s32[]{:S(2)}) async-start(), calls=%async_computation.8 | async-start | bytes 7372800 | tf_op jit(solution)/shard_map/all_gather | solution.py:50
  9.6 96.7 %all-to-all-start = ((bf16[16,48,320]{2,1,0:T(8,128)(2,1)}), bf16[16,48,320]{2,1,0:T(8,128)(2,1)S(1)}, u32[]{:S(2)}, u32[]{:S(2)}) async-start(bf16[16,48,320]{2,1,0:T(8,128)(2,1)} %stack.3), calls=%async_computation | async-start | bytes 1179648 | tf_op jit(solution)/shard_map/all_to_all | solution.py:12
  25.2 511.9 %all-reduce.3.cloned.1.call-start = ((), (), s32[]{:S(2)}) async-start(), calls=%async_computation.5 | async-start | bytes 6291456 | tf_op jit(solution)/shard_map/psum | solution.py:59
  108.1 21.3 %copy-start.1 = (bf16[48,5120]{1,0:T(8,128)(2,1)S(1)}, bf16[48,5120]{1,0:T(8,128)(2,1)}, u32[]{:S(2)}) copy-start(bf16[48,5120]{1,0:T(8,128)(2,1)} %get-tuple-element.8) | copy-start | bytes 1474564
  110.7 23.6 %copy-start.2 = (bf16[48,5120]{1,0:T(8,128)(2,1)}, bf16[48,5120]{1,0:T(8,128)(2,1)S(1)}, u32[]{:S(2)}) copy-start(bf16[48,5120]{1,0:T(8,128)(2,1)S(1)} %get-tuple-element.10) | copy-start | bytes 1474564
  129.4 54.9 %copy-start.6 = (f32[320]{0:T(512)S(1)}, f32[320]{0:T(512)}, u32[]{:S(2)}) copy-start(f32[320]{0:T(512)} %param.10) | copy-start | bytes 3844
  198.6 0.7 copy-start.3
  202.0 0.7 copy-start.7
  202.0 0.7 copy-start.8
  202.0 412.9 %reduce-scatter.6.cloned.1.call-start = ((), (), s32[]{:S(2)}) async-start(), calls=%async_computation.6 | async-start | bytes 331776 | tf_op jit(solution)/shard_map/reduce_scatter | solution.py:71
  573.5 341.5 %reduce-scatter.10.cloned.1.call-start = ((), (), s32[]{:S(2)}) async-start(), calls=%async_computation.9 | async-start | bytes 1392640
  688.2 297.0 %reduce-scatter.8.cloned.1.call-start = ((), (), s32[]{:S(2)}) async-start(), calls=%async_computation.7 | async-start | bytes 1638400 | tf_op jit(solution)/shard_map/reduce_scatter | solution.py:80
  693.3 37.7 %all-to-all-start.1 = ((bf16[48,8,1280]{2,0,1:T(8,128)(2,1)}), bf16[48,8,1280]{2,0,1:T(8,128)(2,1)S(1)}, u32[]{:S(2)}, u32[]{:S(2)}) async-start(bf16[48,8,1280]{2,0,1:T(8,128)(2,1)} %bitcast.69), calls=%async_computation.2 | async-start | bytes 1966080 | tf_op jit(solution)/shard_map/all_to_all | solution.py:49
  731.0 234.6 %copy-start.4 = (bf16[48,320]{1,0:T(8,128)(2,1)S(1)}, bf16[48,320]{1,0:T(8,128)(2,1)}, u32[]{:S(2)}) copy-start(bf16[48,320]{1,0:T(8,128)(2,1)} %reduce-scatter.6.cloned.1.call-done) | copy-start | bytes 92164
Sparse Core Ops, SparseCore 0:
  10.1 119.2 all-gather.3
  202.1 334.9 all-reduce.2
  573.6 41.2 reduce-scatter.5
  688.4 226.5 reduce-scatter.9
  917.7 25.9 reduce-scatter.7
